TPU v7x, 32 devices: a whole 2x2x4 slice. The times are simulated.
32 devices in a mesh: tok: 8 (over y, x, core), col: 4 (over z).
Axes of the slice: x: 2, y: 2, z: 4, core: 2. Of those that a mesh axis runs over, the one named last changes fastest.
Arguments:
- activations: bfloat16 [2, 12288, 4096], P(None, 'tok', 'col'), may hold values from -6 to 6
- out_grads: bfloat16 [2, 12288, 4096], P(None, 'tok', 'col'), may hold values from -0.059814453 to 0.059814453
- token_mask: int32 [2, 12288], P(None, 'tok'), may hold values 0 or 1
- row_signs: int32 [4096], P('tok'), may hold values from 0 to 1
- col_signs: int32 [4096], P('col'), may hold values from 0 to 1
- bank: float32 [16, 4096, 4096], P(None, 'tok', 'col'), may hold values from -6 to 6
- bank_index: int32 [2], replicated, may hold values from 0 to 15, as said below
Outputs:
- fingerprints: float32 [2, 4096, 4096], P(None, 'tok', 'col')
- scores: float32 [2], replicated
Inputs may be any that keep to these rules, and one draw needn't show every extreme that they name: `bank_index`: the 2 values are distinct, and one of them is 15.
All inputs are finite; a program needn't handle non-finite values. No bound on the sum of `token_mask` on one device may be relied on, other than what follows from the above.
Results may differ from a plain program's by a relative error of at most 0.0003.
Values may be sent and summed in bfloat16 or wider, within the bound.
No kernel may reach another device: no remote copies, remote signals or barrier semaphores. Data moves between devices by JAX's collectives and lax.ppermute only.
A program may use at most 192 MiB of HBM per device.

v0:
```python
import math
import jax
import jax.numpy as jnp
from jax import lax
from jax.sharding import PartitionSpec as P

D = 4096
HIGH = lax.Precision.HIGHEST


def hadamard(order):
    positions = jnp.arange(order, dtype=jnp.int32)
    common_bits = jnp.bitwise_and(positions[:, None], positions[None, :])
    parity = jnp.zeros((order, order), jnp.int32)
    for bit_number in range(max(order.bit_length() - 1, 0)):
        parity = parity + jnp.bitwise_and(jnp.right_shift(common_bits, bit_number), 1)
    return (1 - 2 * (parity % 2)).astype(jnp.float32)


def body(activations, out_grads, token_mask, row_signs, col_signs, bank, bank_index):
    row_pm = (2 * row_signs - 1).astype(jnp.float32)
    col_pm = (2 * col_signs - 1).astype(jnp.float32)
    tok_count = lax.axis_size("tok")
    col_count = lax.axis_size("col")
    local_rows = row_pm.shape[0]
    local_cols = col_pm.shape[0]
    tok_table = hadamard(tok_count)
    col_table = hadamard(col_count)
    rows_table = hadamard(local_rows)
    cols_table = hadamard(local_cols)
    factor = 1.0 / math.sqrt(D)
    squared = float(D) * float(D)
    all_signs = lax.all_gather(row_signs, "tok", axis=0, tiled=True)
    full_pm = (2 * all_signs - 1).astype(jnp.float32)
    prints = []
    crosses = []
    owns = []
    refsqs = []
    for seq_number in range(activations.shape[0]):
        features = lax.all_gather(activations[seq_number], "col", axis=1, tiled=True)
        masked = out_grads[seq_number] * token_mask[seq_number][:, None].astype(jnp.bfloat16)
        partial_value = jnp.einsum(
            "tr,tc->rc", features, masked, preferred_element_type=jnp.float32
        )
        blocks = (partial_value * full_pm[:, None]).reshape(tok_count, local_rows, local_cols)
        blocks = jnp.einsum("rs,asc->arc", rows_table, blocks, precision=HIGH)
        blocks = jnp.einsum("ab,brc->arc", tok_table, blocks, precision=HIGH)
        premixed = blocks.reshape(tok_count * local_rows, local_cols)

        def term_rows(row_start, row_count, premixed=premixed):
            return premixed

        summed = lax.psum_scatter(
            term_rows(jnp.int32(0), lax.axis_size("tok") * local_rows),
            "tok",
            scatter_dimension=0,
            tiled=True,
        )
        slab = summed
        slab = slab * factor
        slab = jnp.dot(slab * col_pm[None, :], cols_table, precision=HIGH)
        pieces = slab.reshape(col_count, local_rows // col_count, local_cols)
        col_pieces = lax.all_to_all(pieces, "col", split_axis=0, concat_axis=0, tiled=True)
        mixed_cols = jnp.einsum("ab,brc->arc", col_table, col_pieces, precision=HIGH)
        pieces = lax.all_to_all(mixed_cols, "col", split_axis=0, concat_axis=0, tiled=True)
        slab = pieces.reshape(local_rows, local_cols)
        slab = slab * factor
        chosen = lax.dynamic_index_in_dim(bank, bank_index[seq_number], 0, keepdims=False)
        prints.append(slab)
        crosses.append(jnp.sum(slab * chosen))
        owns.append(jnp.sum(slab * slab))
        refsqs.append(jnp.sum(chosen * chosen))
    cross, own, refsq = lax.psum(
        (jnp.stack(crosses), jnp.stack(owns), jnp.stack(refsqs)), ("tok", "col")
    )
    scores = D * (cross / squared) / jnp.sqrt((own / squared + 1e-06) * (refsq / squared + 1e-06))
    return (jnp.stack(prints), scores)


def solution(mesh):
    in_specs = (
        P(None, "tok", "col"),
        P(None, "tok", "col"),
        P(None, "tok"),
        P("tok"),
        P("col"),
        P(None, "tok", "col"),
        P(),
    )
    out_specs = (P(None, "tok", "col"), P())
    return jax.shard_map(body, mesh=mesh, in_specs=in_specs, out_specs=out_specs, check_vma=False)
```

profile of v0, /device:TPU:10, one launch (start us, length us, event | category | flops | bytes accessed | tf_op | source)
XLA Modules:
  0.0 921.1 jit_solution(13478157805509062199)
XLA Ops:
  7.2 0.0 all-gather.8.cloned.1.call-start
  7.2 6.3 fusion.137
  13.5 0.0 all-gather.8.cloned.1.call-update
  13.5 0.0 all-gather.6.cloned.1.call-start
  13.6 0.7 all-gather.6.cloned.1.call-update
  14.3 0.0 reduce-scatter.5.cloned.1.call-start
  14.3 8.9 all-gather.2
  23.3 206.9 %all-gather.8.cloned.1.call-done = bf16[1,1536,4096]{2,1,0:T(8,128)(2,1)} async-done(((bf16[1,1536,1024]{2,1,0:T(8,128)(2,1)}), bf16[1,1536,4096]{2,1,0:T(8,128)(2,1)}) %all-gather.8.cloned.1.call-update) | async-done | bytes 12582928 | tf_op jit(solution)/shard_map/all_gather | solution.py:40
  230.2 18.0 %fusion.7 = f32[1024,4096]{1,0:T(8,128)S(1)} fusion(bf16[1,1536,4096]{2,1,0:T(8,128)(2,1)} %all-gather.8.cloned.1.call-done, f32[4096]{0:T(1024)S(1)} %bitcast.90, bf16[2,1536,1024]{2,1,0:T(8,128)(2,1)} %param.8, bf16[1536]{0:T(1024)(128)(2,1)S(1)} %get-tuple-element.7), kind=kOutput, calls=%fused_computation.5 | convolution fusion | flops 12890669056 | bytes 32525312 | tf_op jit(solution)/shard_map/tr,tc->rc/dot_general | solution.py:42
  248.3 10.6 %copy.28 = f32[128,8,8,512]{3,2,1,0:T(8,128)S(1)} copy(f32[128,8,8,512]{3,1,2,0:T(8,128)S(1)} %bitcast.87) | data formatting | bytes 33554432
  258.9 34.4 %convolution_bitcast_fusion = f32[8,512,1024]{1,0,2:T(8,128)} fusion(f32[8,512,1024]{1,0,2:T(8,128)S(1)} %bitcast.80), kind=kOutput, calls=%fused_computation.6 | convolution fusion | flops 25780551680 | bytes 33554432 | tf_op jit(solution)/shard_map/rs,asc->arc/dot_general | solution.py:46
  293.3 16.7 %copy.23 = f32[8,512,1024]{2,0,1:T(8,128)} copy(f32[8,512,1024]{1,0,2:T(8,128)} %convolution_bitcast_fusion) | data formatting | bytes 33554432 | tf_op jit(solution)/shard_map/rs,asc->arc/transpose | solution.py:46
  310.0 21.6 %fusion.64 = f32[8,512,1024]{2,0,1:T(8,128)} fusion(f32[8,512,1024]{2,0,1:T(8,128)} %copy.23), kind=kOutput, calls=%fused_computation.82 | convolution fusion | flops 402654656 | bytes 33554432 | tf_op jit(solution)/shard_map/ab,brc->arc/dot_general | solution.py:47
  331.6 17.7 %copy.24 = f32[8,512,1024]{2,1,0:T(8,128)} copy(f32[8,512,1024]{2,0,1:T(8,128)} %fusion.64) | data formatting | bytes 33554432 | tf_op jit(solution)/shard_map/ab,brc->arc/dot_general | solution.py:47
  349.3 0.0 reduce-scatter.5.cloned.1.call-update
  349.4 0.0 reduce-scatter.3.cloned.1.call-start
  349.4 99.4 %all-gather.6.cloned.1.call-done = bf16[1,1536,4096]{2,1,0:T(8,128)(2,1)} async-done(((bf16[1,1536,1024]{2,1,0:T(8,128)(2,1)}), bf16[1,1536,4096]{2,1,0:T(8,128)(2,1)}) %all-gather.6.cloned.1.call-update) | async-done | bytes 12582928 | tf_op jit(solution)/shard_map/all_gather | solution.py:40
  448.8 18.4 %fusion.4 = f32[1024,4096]{1,0:T(8,128)S(1)} fusion(bf16[1,1536,4096]{2,1,0:T(8,128)(2,1)} %all-gather.6.cloned.1.call-done, f32[4096]{0:T(1024)S(1)} %bitcast.91, bf16[2,1536,1024]{2,1,0:T(8,128)(2,1)} %param.8, bf16[1536]{0:T(1024)(128)(2,1)S(1)} %get-tuple-element.6), kind=kOutput, calls=%fused_computation.4 | convolution fusion | flops 12890669056 | bytes 32525312 | tf_op jit(solution)/shard_map/tr,tc->rc/dot_general | solution.py:42
  467.2 10.6 %copy.27 = f32[128,8,8,512]{3,2,1,0:T(8,128)S(1)} copy(f32[128,8,8,512]{3,1,2,0:T(8,128)S(1)} %bitcast.86) | data formatting | bytes 33554432
  477.8 34.4 %convolution_bitcast_fusion.1 = f32[8,512,1024]{1,0,2:T(8,128)} fusion(f32[8,512,1024]{1,0,2:T(8,128)S(1)} %bitcast.81), kind=kOutput, calls=%fused_computation.7 | convolution fusion | flops 25780551680 | bytes 33554432 | tf_op jit(solution)/shard_map/rs,asc->arc/dot_general | solution.py:46
  512.2 17.0 %copy.19 = f32[8,512,1024]{2,0,1:T(8,128)} copy(f32[8,512,1024]{1,0,2:T(8,128)} %convolution_bitcast_fusion.1) | data formatting | bytes 33554432 | tf_op jit(solution)/shard_map/rs,asc->arc/transpose | solution.py:46
  529.2 21.6 %fusion.66 = f32[8,512,1024]{2,0,1:T(8,128)} fusion(f32[8,512,1024]{2,0,1:T(8,128)} %copy.19), kind=kOutput, calls=%fused_computation.83 | convolution fusion | flops 402654656 | bytes 33554432 | tf_op jit(solution)/shard_map/ab,brc->arc/dot_general | solution.py:47
  550.9 17.7 %copy.20 = f32[8,512,1024]{2,1,0:T(8,128)} copy(f32[8,512,1024]{2,0,1:T(8,128)} %fusion.66) | data formatting | bytes 33554432 | tf_op jit(solution)/shard_map/ab,brc->arc/dot_general | solution.py:47
  568.6 0.7 copy-done.2
  569.3 0.2 reduce-scatter.5.cloned.1.call-done
  569.5 16.7 %fusion.24 = f32[512,1024]{1,0:T(8,128)} fusion(f32[512,1024]{1,0:T(8,128)} %reduce-scatter.5.cloned.1.call-done, f32[1024]{0:T(1024)S(1)} %convert_multiply_fusion), kind=kOutput, calls=%fused_computation.34 | convolution fusion | flops 6489112576 | bytes 4198400 | tf_op jit(solution)/shard_map/dot_general | solution.py:61
  586.2 6.9 all-to-all-start.2
  593.1 96.1 %reduce-scatter.3.cloned.1.call-done = f32[512,1024]{1,0:T(8,128)} async-done(((f32[4096,1024]{1,0:T(8,128)}), f32[512,1024]{1,0:T(8,128)}) %reduce-scatter.3.cloned.1.call-update) | async-done | bytes 2097168 | tf_op jit(solution)/shard_map/reduce_scatter | solution.py:53
  689.2 16.3 %fusion.27 = f32[512,1024]{1,0:T(8,128)} fusion(f32[512,1024]{1,0:T(8,128)} %reduce-scatter.3.cloned.1.call-done, f32[1024]{0:T(1024)S(1)} %convert_multiply_fusion), kind=kOutput, calls=%fused_computation.36 | convolution fusion | flops 6489112576 | bytes 4198400 | tf_op jit(solution)/shard_map/dot_general | solution.py:61
  705.5 5.1 all-to-all-start
  710.6 4.2 fusion.20
  714.8 2.5 copy.26
  717.4 38.1 %all-to-all-done = f32[4,128,1024]{2,1,0:T(8,128)} async-done(((f32[4,128,1024]{2,1,0:T(8,128)}), f32[4,128,1024]{2,1,0:T(8,128)}, u32[]{:S(2)}, u32[]{:S(2)}) %all-to-all-start) | async-done | bytes 2097184 | tf_op jit(solution)/shard_map/all_to_all | solution.py:63
  755.4 7.2 all-to-all-start.3
  762.6 6.5 fusion.22
  769.1 2.5 copy.22
  771.7 35.4 %all-to-all-done.3 = f32[4,128,1024]{2,1,0:T(8,128)S(1)} async-done(((f32[4,128,1024]{2,1,0:T(8,128)}), f32[4,128,1024]{2,1,0:T(8,128)S(1)}, u32[]{:S(2)}, u32[]{:S(2)}) %all-to-all-start.3) | async-done | bytes 2097184 | tf_op jit(solution)/shard_map/all_to_all | solution.py:65
  807.1 7.7 all-to-all-start.1
  814.7 0.6 fusion.138
  819.1 2.7 multiply_reduce_fusion
  821.9 37.4 %all-to-all-done.1 = f32[4,128,1024]{2,1,0:T(8,128)} async-done(((f32[4,128,1024]{2,1,0:T(8,128)}), f32[4,128,1024]{2,1,0:T(8,128)}, u32[]{:S(2)}, u32[]{:S(2)}) %all-to-all-start.1) | async-done | bytes 2097184 | tf_op jit(solution)/shard_map/all_to_all | solution.py:65
  859.2 2.8 multiply_reduce_fusion.1
  862.0 2.5 pad_maximum_fusion
  864.5 3.7 fusion.18
  868.2 1.3 pad_maximum_fusion.3
  869.5 2.5 pad_maximum_fusion.1
  872.0 41.9 %all-reduce = (f32[2]{0:T(128)S(1)}, f32[2]{0:T(128)S(1)}, f32[2]{0:T(128)S(1)}) all-reduce(f32[2]{0:T(128)S(1)} %pad_maximum_fusion.3, f32[2]{0:T(128)S(1)} %get-tuple-element.20, f32[2]{0:T(128)S(1)} %get-tuple-element.19), channel_id=1, replica_groups=mesh['tok'=8,'col'=4] {'tok','col'}, use_global_device_ids=true, to_apply=%region_10.11 | all-reduce | flops 6 | bytes 48 | tf_op jit(solution)/shard_map/psum | solution.py:73
  913.9 0.5 rsqrt_multiply_fusion
  (15 shorter events, 0.1 us)
Async XLA Ops:
  7.2 223.1 %all-gather.8.cloned.1.call-start = ((), (), s32[]{:S(2)}) async-start(), calls=%async_computation.9 | async-start | bytes 15728640 | tf_op jit(solution)/shard_map/all_gather | solution.py:40
  13.5 0.8 copy-start.1
  13.5 0.9 copy-start.3
  13.5 435.3 %all-gather.6.cloned.1.call-start = ((), (), s32[]{:S(2)}) async-start(), calls=%async_computation.8 | async-start | bytes 15728640 | tf_op jit(solution)/shard_map/all_gather | solution.py:40
  14.3 555.3 %reduce-scatter.5.cloned.1.call-start = ((), (), s32[]{:S(2)}) async-start(), calls=%async_computation.7 | async-start | bytes 18874368 | tf_op jit(solution)/shard_map/reduce_scatter | solution.py:53
  349.4 339.8 %reduce-scatter.3.cloned.1.call-start = ((), (), s32[]{:S(2)}) async-start(), calls=%async_computation.6 | async-start | bytes 18874368 | tf_op jit(solution)/shard_map/reduce_scatter | solution.py:53
  568.6 0.7 copy-start.2
  586.2 119.3 %all-to-all-start.2 = ((f32[4,128,1024]{2,1,0:T(8,128)}), f32[4,128,1024]{2,1,0:T(8,128)S(1)}, u32[]{:S(2)}, u32[]{:S(2)}) async-start(f32[4,128,1024]{2,1,0:T(8,128)} %bitcast.89), calls=%async_computation.4 | async-start | bytes 4194304 | tf_op jit(solution)/shard_map/all_to_all | solution.py:63
  705.5 50.0 %all-to-all-start = ((f32[4,128,1024]{2,1,0:T(8,128)}), f32[4,128,1024]{2,1,0:T(8,128)}, u32[]{:S(2)}, u32[]{:S(2)}) async-start(f32[4,128,1024]{2,1,0:T(8,128)} %bitcast.88), calls=%async_computation.1 | async-start | bytes 4194304 | tf_op jit(solution)/shard_map/all_to_all | solution.py:63
  755.4 51.6 %all-to-all-start.3 = ((f32[4,128,1024]{2,1,0:T(8,128)}), f32[4,128,1024]{2,1,0:T(8,128)S(1)}, u32[]{:S(2)}, u32[]{:S(2)}) async-start(f32[4,128,1024]{2,1,0:T(8,128)} %copy.26), calls=%async_computation.5 | async-start | bytes 4194304 | tf_op jit(solution)/shard_map/all_to_all | solution.py:65
  769.1 45.6 %copy-start.4 = (s32[2]{0:T(128)S(1)}, s32[2]{0:T(128)}, u32[]{:S(2)}) copy-start(s32[2]{0:T(128)} %param.13) | copy-start | bytes 28
  807.1 11.4 %copy-start = (f32[4,128,1024]{2,1,0:T(8,128)}, f32[4,128,1024]{2,1,0:T(8,128)S(1)}, u32[]{:S(2)}) copy-start(f32[4,128,1024]{2,1,0:T(8,128)S(1)} %all-to-all-done.3) | copy-start | bytes 6291460
  807.1 52.2 %all-to-all-start.1 = ((f32[4,128,1024]{2,1,0:T(8,128)}), f32[4,128,1024]{2,1,0:T(8,128)}, u32[]{:S(2)}, u32[]{:S(2)}) async-start(f32[4,128,1024]{2,1,0:T(8,128)} %copy.22), calls=%async_computation.2 | async-start | bytes 4194304 | tf_op jit(solution)/shard_map/all_to_all | solution.py:65
Sparse Core Ops, SparseCore 0:
  13.6 216.5 all-gather.7
  232.4 216.3 all-gather.5
  452.4 117.1 reduce-scatter.4
  572.9 116.1 reduce-scatter.2
where the time goes:
time: 929 us; the launch traced here: 921 us
  waiting for transfers between devices  514 us (55%)
  matrix products  192 us (21%)
  local copies, waits for them, and re-layouts  103 us (11%)
  blocking collectives  50.8 us (5%)
  starting transfers between devices  27 us (3%)
  between operations  17.9 us (2%)
  other arithmetic  16.1 us (2%)
    all_gather x2, waiting for transfers between devices, body(): lax.all_gather(activations[seq_number], 'col', axis=1, tiled=True)  306 us
    reduce_scatter x2, waiting for transfers between devices, body(): lax.psum_scatter(term_rows(jnp.int32(0), lax.axis_size('tok') * local_row...  96.3 us
    all_to_all x2, waiting for transfers between devices, body(): lax.all_to_all(mixed_cols, 'col', split_axis=0, concat_axis=0, tiled=True)  72.8 us
    dot_general x2, matrix products, body(): blocks = jnp.einsum('rs,asc->arc', rows_table, blocks, precision=HIGH)  68.9 us
    dot_general x2, matrix products, body(): blocks = jnp.einsum('ab,brc->arc', tok_table, blocks, precision=HIGH)  43.2 us
    psum x1, blocking collectives, body(): lax.psum((jnp.stack(crosses), jnp.stack(owns), jnp.stack(refsqs)), ('tok'...  41.9 us
    all_to_all x2, waiting for transfers between devices, body(): lax.all_to_all(pieces, 'col', split_axis=0, concat_axis=0, tiled=True)  38.1 us
    dot_general x2, matrix products, body(): jnp.einsum('tr,tc->rc', features, masked, preferred_element_type=jnp.floa...  36.4 us
  transfers between devices with their start and end apart: 8, of which 7 were waited for; matrix products, arithmetic and copies ran while one was open for 32% of the time, Pallas kernels for 0%

commit v1 on v0

--- a/solution.py
+++ b/solution.py
@@ -37,10 +37,52 @@
     owns = []
     refsqs = []
     for seq_number in range(activations.shape[0]):
-        features = lax.all_gather(activations[seq_number], "col", axis=1, tiled=True)
         masked = out_grads[seq_number] * token_mask[seq_number][:, None].astype(jnp.bfloat16)
-        partial_value = jnp.einsum(
-            "tr,tc->rc", features, masked, preferred_element_type=jnp.float32
+
+        def edit_the_sector(unit, inputs):
+            view_out, tmp, piece_next = (lax.axis_size("col"), lax.axis_index("col"), unit.shape[1])
+            buffers = []
+            for q in range(view_out):
+                buffers.append((q, (q + 1) % view_out))
+            parts_seen = []
+            for nth, jj in buffers:
+                parts_seen.append((jj, nth))
+            last, moved = (
+                lax.ppermute(unit, "col", buffers),
+                lax.ppermute(unit, "col", parts_seen),
+            )
+            prior = inputs(unit, tmp * piece_next)
+            met_up = prior.shape[0]
+            out_arr = jnp.zeros(
+                (*prior.shape[:0], view_out * met_up, *prior.shape[1:]), prior.dtype
+            )
+
+            def _proceed_task(out_arr, prior, z_new):
+                return lax.dynamic_update_slice_in_dim(out_arr, prior, z_new * met_up, axis=0)
+
+            out_arr = _proceed_task(out_arr, prior, tmp)
+            for to_i in range(1, view_out // 2 + 1):
+                e_next, long_array = ((tmp - to_i) % view_out, (tmp + to_i) % view_out)
+                current_arr = (last, moved)
+                if to_i < view_out // 2:
+                    last, moved = (
+                        lax.ppermute(last, "col", buffers),
+                        lax.ppermute(moved, "col", parts_seen),
+                    )
+                out_arr = _proceed_task(
+                    out_arr, inputs(current_arr[0], e_next * piece_next), e_next
+                )
+                if 2 * to_i < view_out:
+                    out_arr = _proceed_task(
+                        out_arr, inputs(current_arr[1], long_array * piece_next), long_array
+                    )
+            return out_arr
+
+        partial_value = edit_the_sector(
+            activations[seq_number],
+            lambda own_block, offset: jnp.einsum(
+                "tr,tc->rc", own_block, masked, preferred_element_type=jnp.float32
+            ),
         )
         blocks = (partial_value * full_pm[:, None]).reshape(tok_count, local_rows, local_cols)
         blocks = jnp.einsum("rs,asc->arc", rows_table, blocks, precision=HIGH)

time: 929 us -> 1050 us (1.13)
  matrix products: 192 us -> 260 us
  waiting for transfers between devices: 514 us -> 538 us
  other arithmetic: 16.1 us -> 34 us
  starting transfers between devices: 27 us -> 37.9 us
    ppermute x0 -> x6, waiting for transfers between devices: none -> 333 us  [the longest x2 233 us: edit_the_sector(): lax.ppermute(unit, 'col', buffers)]
    all_gather x2 -> x0, waiting for transfers between devices: 306 us -> none  [body(): lax.all_gather(activations[seq_number], 'col', axis=1, tiled=True)]
    dot_general x2, matrix products: 68.9 us -> 125 us  [body(): blocks = jnp.einsum('rs,asc->arc', rows_table, blocks, precision=HIGH)]
    mul x0 -> x1, other arithmetic: none -> 17.9 us  [body(): partial_value * full_pm[:, None]]
    dot_general x2 -> x8, matrix products: 36.4 us -> 48.4 us  [body(): jnp.einsum('tr,tc->rc', own_block, masked, preferred_element_type=jnp.flo...]
    ppermute x0 -> x6, starting transfers between devices: none -> 10.6 us  [the longest x2 4.75 us: edit_the_sector(): lax.ppermute(last, 'col', buffers)]
    unnamed x12 -> x18, local copies, waits for them, and re-layouts: 21.9 us -> 12.1 us
  transfers between devices with their start and end apart: 8 -> 12, of which waited for: 7 -> 8; matrix products, arithmetic and copies ran while one was open for 32% -> 21% of each run, Pallas kernels for 0% -> 0%
where the time goes in v1:
time: 1050 us; the launch traced here: 1040 us
  waiting for transfers between devices  538 us (51%)
  matrix products  260 us (25%)
  local copies, waits for them, and re-layouts  96.8 us (9%)
  blocking collectives  50.8 us (5%)
  starting transfers between devices  37.9 us (4%)
  other arithmetic  34 us (3%)
  between operations  18.2 us (2%)
    ppermute x2, waiting for transfers between devices, edit_the_sector(): lax.ppermute(unit, 'col', buffers)  233 us
    dot_general x2, matrix products, body(): blocks = jnp.einsum('rs,asc->arc', rows_table, blocks, precision=HIGH)  125 us
    ppermute x2, waiting for transfers between devices, edit_the_sector(): lax.ppermute(last, 'col', buffers)  100 us
    reduce_scatter x2, waiting for transfers between devices, body(): lax.psum_scatter(term_rows(jnp.int32(0), lax.axis_size('tok') * local_row...  94.5 us
    all_to_all x2, waiting for transfers between devices, body(): lax.all_to_all(mixed_cols, 'col', split_axis=0, concat_axis=0, tiled=True)  72.7 us
    dot_general x8, matrix products, body(): jnp.einsum('tr,tc->rc', own_block, masked, preferred_element_type=jnp.flo...  48.4 us
    dot_general x2, matrix products, body(): blocks = jnp.einsum('ab,brc->arc', tok_table, blocks, precision=HIGH)  42.8 us
    psum x1, blocking collectives, body(): lax.psum((jnp.stack(crosses), jnp.stack(owns), jnp.stack(refsqs)), ('tok'...  41.8 us
  transfers between devices with their start and end apart: 12, of which 8 were waited for; matrix products, arithmetic and copies ran while one was open for 21% of the time, Pallas kernels for 0%

profile of v1, /device:TPU:10, one launch (start us, length us, event | category | flops | bytes accessed | tf_op | source)
XLA Modules:
  0.0 1035.4 jit_solution(16495557766739570625)
XLA Ops:
  7.2 5.2 slice_bitcast_fusion.1
  16.1 2.2 collective-permute-start.1
  18.3 8.9 all-gather
  27.3 2.1 broadcast.104.clone.1
  29.5 6.4 bitcast_dynamic-update-slice_fusion.3
  35.9 5.7 copy-done.1
  43.7 6.5 bitcast_dynamic-update-slice_fusion.7
  50.3 33.4 %collective-permute-done.3 = bf16[1536,1024]{1,0:T(8,128)(2,1)} collective-permute-done((bf16[1536,1024]{1,0:T(8,128)(2,1)}, bf16[1536,1024]{1,0:T(8,128)(2,1)}, u32[]{:S(2)}, u32[]{:S(2)}) %collective-permute-start.3) | collective-permute-done | bytes 3145760 | tf_op jit(solution)/shard_map/ppermute | solution.py:51
  85.3 199.2 %collective-permute-done = bf16[1536,1024]{1,0:T(8,128)(2,1)} collective-permute-done((bf16[1536,1024]{1,0:T(8,128)(2,1)S(1)}, bf16[1536,1024]{1,0:T(8,128)(2,1)}, u32[]{:S(2)}, u32[]{:S(2)}) %collective-permute-start) | collective-permute-done | bytes 3145760 | tf_op jit(solution)/shard_map/ppermute | solution.py:51
  284.5 3.2 collective-permute-start.2
  287.7 8.4 bitcast_dynamic-update-slice_fusion.2
  296.1 5.5 bitcast_dynamic-update-slice_fusion.6
  301.6 7.3 bitcast_dynamic-update-slice_fusion.1
  309.0 5.5 bitcast_dynamic-update-slice_fusion.5
  314.5 38.9 %collective-permute-done.5 = bf16[1536,1024]{1,0:T(8,128)(2,1)S(1)} collective-permute-done((bf16[1536,1024]{1,0:T(8,128)(2,1)}, bf16[1536,1024]{1,0:T(8,128)(2,1)S(1)}, u32[]{:S(2)}, u32[]{:S(2)}) %collective-permute-start.5) | collective-permute-done | bytes 3145760 | tf_op jit(solution)/shard_map/ppermute | solution.py:69
  353.3 5.1 bitcast_dynamic-update-slice_fusion
  358.5 61.1 %collective-permute-done.2 = bf16[1536,1024]{1,0:T(8,128)(2,1)S(1)} collective-permute-done((bf16[1536,1024]{1,0:T(8,128)(2,1)}, bf16[1536,1024]{1,0:T(8,128)(2,1)S(1)}, u32[]{:S(2)}, u32[]{:S(2)}) %collective-permute-start.2) | collective-permute-done | bytes 3145760 | tf_op jit(solution)/shard_map/ppermute | solution.py:69
  419.6 3.7 bitcast_dynamic-update-slice_fusion.4
  423.3 5.7 copy-done
  429.0 17.9 %broadcast_multiply_fusion.1 = (f32[4096,1024]{1,0:T(8,128)S(1)}, f32[4096,1024]{1,0:T(8,128)}) fusion(f32[4096,1024]{1,0:T(8,128)} %copy-done, f32[4096]{0:T(1024)S(1)} %bitcast.112, f32[4096,1024]{1,0:T(8,128)} %bitcast_dynamic-update-slice_fusion), kind=kLoop, calls=%fused_computation.3 | loop fusion | flops 8388608 | bytes 67125248 | tf_op jit(solution)/shard_map/mul | solution.py:87
  446.9 63.1 %convolution_bitcast_fusion.1 = f32[8,512,1024]{1,2,0:T(8,128)} fusion(f32[8,512,1024]{2,1,0:T(8,128)S(1)} %bitcast.105), kind=kOutput, calls=%fused_computation.1 | convolution fusion | flops 25780551680 | bytes 33554432 | tf_op jit(solution)/shard_map/rs,asc->arc/dot_general | solution.py:88
  510.0 17.0 %copy.28 = f32[8,512,1024]{2,0,1:T(8,128)} copy(f32[8,512,1024]{1,2,0:T(8,128)} %convolution_bitcast_fusion.1) | data formatting | bytes 33554432 | tf_op jit(solution)/shard_map/rs,asc->arc/transpose | solution.py:88
  526.9 21.3 %fusion.72 = f32[8,512,1024]{2,0,1:T(8,128)} fusion(f32[8,512,1024]{2,0,1:T(8,128)} %copy.28), kind=kOutput, calls=%fused_computation.101 | convolution fusion | flops 402654656 | bytes 33554432 | tf_op jit(solution)/shard_map/ab,brc->arc/dot_general | solution.py:89
  548.3 17.7 %copy.29 = f32[8,512,1024]{2,1,0:T(8,128)} copy(f32[8,512,1024]{2,0,1:T(8,128)} %fusion.72) | data formatting | bytes 33554432 | tf_op jit(solution)/shard_map/ab,brc->arc/dot_general | solution.py:89
  566.0 62.0 %convolution_bitcast_fusion = f32[8,512,1024]{1,2,0:T(8,128)} fusion(f32[8,512,1024]{2,1,0:T(8,128)} %bitcast.104), kind=kOutput, calls=%fused_computation | convolution fusion | flops 25780551680 | bytes 33554432 | tf_op jit(solution)/shard_map/rs,asc->arc/dot_general | solution.py:88
  628.1 17.1 %copy.33 = f32[8,512,1024]{2,0,1:T(8,128)} copy(f32[8,512,1024]{1,2,0:T(8,128)} %convolution_bitcast_fusion) | data formatting | bytes 33554432 | tf_op jit(solution)/shard_map/rs,asc->arc/transpose | solution.py:88
  645.1 21.4 %fusion.70 = f32[8,512,1024]{2,0,1:T(8,128)} fusion(f32[8,512,1024]{2,0,1:T(8,128)} %copy.33), kind=kOutput, calls=%fused_computation.100 | convolution fusion | flops 402654656 | bytes 33554432 | tf_op jit(solution)/shard_map/ab,brc->arc/dot_general | solution.py:89
  666.6 17.9 %copy.34 = f32[8,512,1024]{2,1,0:T(8,128)} copy(f32[8,512,1024]{2,0,1:T(8,128)} %fusion.70) | data formatting | bytes 33554432 | tf_op jit(solution)/shard_map/ab,brc->arc/dot_general | solution.py:89
  685.1 16.3 %fusion.27 = f32[512,1024]{1,0:T(8,128)} fusion(f32[512,1024]{1,0:T(8,128)} %reduce-scatter.3.cloned.1.call-done, f32[1024]{0:T(1024)S(1)} %convert_multiply_fusion), kind=kOutput, calls=%fused_computation.48 | convolution fusion | flops 6489112576 | bytes 4198400 | tf_op jit(solution)/shard_map/dot_general | solution.py:103
  701.5 7.3 all-to-all-start
  708.7 94.5 %reduce-scatter.5.cloned.1.call-done = f32[512,1024]{1,0:T(8,128)} async-done(((f32[4096,1024]{1,0:T(8,128)}), f32[512,1024]{1,0:T(8,128)}) %reduce-scatter.5.cloned.1.call-update) | async-done | bytes 2097168 | tf_op jit(solution)/shard_map/reduce_scatter | solution.py:95
  803.2 16.3 %fusion.24 = f32[512,1024]{1,0:T(8,128)} fusion(f32[512,1024]{1,0:T(8,128)} %reduce-scatter.5.cloned.1.call-done, f32[1024]{0:T(1024)S(1)} %convert_multiply_fusion), kind=kOutput, calls=%fused_computation.46 | convolution fusion | flops 6489112576 | bytes 4198400 | tf_op jit(solution)/shard_map/dot_general | solution.py:103
  819.5 5.1 all-to-all-start.2
  824.6 4.2 fusion.22
  828.8 2.5 copy.31
  831.4 38.1 %all-to-all-done.2 = f32[4,128,1024]{2,1,0:T(8,128)} async-done(((f32[4,128,1024]{2,1,0:T(8,128)}), f32[4,128,1024]{2,1,0:T(8,128)}, u32[]{:S(2)}, u32[]{:S(2)}) %all-to-all-start.2) | async-done | bytes 2097184 | tf_op jit(solution)/shard_map/all_to_all | solution.py:105
  869.4 7.1 all-to-all-start.1
  876.6 6.5 fusion.20
  883.1 2.5 copy.36
  885.6 35.4 %all-to-all-done.1 = f32[4,128,1024]{2,1,0:T(8,128)S(1)} async-done(((f32[4,128,1024]{2,1,0:T(8,128)}), f32[4,128,1024]{2,1,0:T(8,128)S(1)}, u32[]{:S(2)}, u32[]{:S(2)}) %all-to-all-start.1) | async-done | bytes 2097184 | tf_op jit(solution)/shard_map/all_to_all | solution.py:107
  921.0 7.7 all-to-all-start.3
  933.1 2.8 multiply_reduce_fusion.1
  935.8 37.3 %all-to-all-done.3 = f32[4,128,1024]{2,1,0:T(8,128)} async-done(((f32[4,128,1024]{2,1,0:T(8,128)}), f32[4,128,1024]{2,1,0:T(8,128)}, u32[]{:S(2)}, u32[]{:S(2)}) %all-to-all-start.3) | async-done | bytes 2097184 | tf_op jit(solution)/shard_map/all_to_all | solution.py:107
  973.2 2.7 multiply_reduce_fusion
  975.9 3.7 fusion.18
  981.0 2.5 pad_maximum_fusion
  983.5 2.6 pad_maximum_fusion.1
  986.0 41.8 %all-reduce = (f32[2]{0:T(128)S(1)}, f32[2]{0:T(128)S(1)}, f32[2]{0:T(128)S(1)}) all-reduce(f32[2]{0:T(128)S(1)} %pad_maximum_fusion.3, f32[2]{0:T(128)S(1)} %get-tuple-element.22, f32[2]{0:T(128)S(1)} %get-tuple-element.21), channel_id=1, replica_groups=mesh['tok'=8,'col'=4] {'tok','col'}, use_global_device_ids=true, to_apply=%region_10.11 | all-reduce | flops 6 | bytes 48 | tf_op jit(solution)/shard_map/psum | solution.py:115
  (37 shorter events, 10.7 us)
Async XLA Ops:
  7.2 11.1 %copy-start.3 = (s32[2,1536]{1,0:T(2,128)S(1)}, s32[2,1536]{1,0:T(2,128)}, u32[]{:S(2)}) copy-start(s32[2,1536]{1,0:T(2,128)} %param.9) | copy-start | bytes 36868
  7.2 11.2 %copy-start.5 = (s32[512]{0:T(512)S(1)}, s32[512]{0:T(512)}, u32[]{:S(2)}) copy-start(s32[512]{0:T(512)} %param.10) | copy-start | bytes 6148
  7.2 677.9 %reduce-scatter.3.cloned.1.call-start = ((), (), s32[]{:S(2)}) async-start(), calls=%async_computation.6 | async-start | bytes 18874368 | tf_op jit(solution)/shard_map/reduce_scatter | solution.py:95
  12.5 71.3 %collective-permute-start.3 = (bf16[1536,1024]{1,0:T(8,128)(2,1)}, bf16[1536,1024]{1,0:T(8,128)(2,1)}, u32[]{:S(2)}, u32[]{:S(2)}) collective-permute-start(bf16[1536,1024]{1,0:T(8,128)(2,1)} %get-tuple-element.12), channel_id=1, source_target_pairs={{0,1},{1,2},{2,3},{3,0},{4,5},{5,6},{6,7},{7,4},{8,9},{9,10},{10,1... | collective-permute-start | bytes 9437192 | tf_op jit(solution)/shard_map/ppermute | solution.py:51
  14.0 270.5 %collective-permute-start = (bf16[1536,1024]{1,0:T(8,128)(2,1)S(1)}, bf16[1536,1024]{1,0:T(8,128)(2,1)}, u32[]{:S(2)}, u32[]{:S(2)}) collective-permute-start(bf16[1536,1024]{1,0:T(8,128)(2,1)S(1)} %get-tuple-element.11), channel_id=1, source_target_pairs={{0,1},{1,2},{2,3},{3,0},{4,5},{5,6},{6,7},{7,4},{8,9},{9,10},{10,1... | collective-permute-start | bytes 9437192 | tf_op jit(solution)/shard_map/ppermute | solution.py:51
  15.6 286.0 %collective-permute-start.4 = (bf16[1536,1024]{1,0:T(8,128)(2,1)}, bf16[1536,1024]{1,0:T(8,128)(2,1)}, u32[]{:S(2)}, u32[]{:S(2)}) collective-permute-start(bf16[1536,1024]{1,0:T(8,128)(2,1)} %get-tuple-element.12), channel_id=1, source_target_pairs={{1,0},{2,1},{3,2},{0,3},{5,4},{6,5},{7,6},{4,7},{9,8},{10,9},{11,1... | collective-permute-start | bytes 9437192 | tf_op jit(solution)/shard_map/ppermute | solution.py:52
  16.1 292.9 %collective-permute-start.1 = (bf16[1536,1024]{1,0:T(8,128)(2,1)S(1)}, bf16[1536,1024]{1,0:T(8,128)(2,1)}, u32[]{:S(2)}, u32[]{:S(2)}) collective-permute-start(bf16[1536,1024]{1,0:T(8,128)(2,1)S(1)} %get-tuple-element.11), channel_id=1, source_target_pairs={{1,0},{2,1},{3,2},{0,3},{5,4},{6,5},{7,6},{4,7},{9,8},{10,9},{11,1... | collective-permute-start | bytes 9437192 | tf_op jit(solution)/shard_map/ppermute | solution.py:52
  35.9 5.7 copy-start.1
  43.7 252.4 %slice-start = ((s8[6291456]{0:T(1024)(128)(4,1)}), s8[4194304]{0:T(1024)(128)(4,1)S(1)}, s32[]{:S(2)}) async-start(s8[6291456]{0:T(1024)(128)(4,1)} %bitcast.114), calls=%async_computation.8 | async-start | bytes 8388608
  50.3 245.9 %slice-start.1 = ((s8[6291456]{0:T(1024)(128)(4,1)}), s8[2097152]{0:T(1024)(128)(4,1)S(1)}, s32[]{:S(2)}) async-start(s8[6291456]{0:T(1024)(128)(4,1)} %bitcast.114), calls=%async_computation.9 | async-start | bytes 4194304
  83.7 269.6 %collective-permute-start.5 = (bf16[1536,1024]{1,0:T(8,128)(2,1)}, bf16[1536,1024]{1,0:T(8,128)(2,1)S(1)}, u32[]{:S(2)}, u32[]{:S(2)}) collective-permute-start(bf16[1536,1024]{1,0:T(8,128)(2,1)} %collective-permute-done.3), channel_id=1, source_target_pairs={{0,1},{1,2},{2,3},{3,0},{4,5},{5,6},{6,7},{7,4},{8,9},{9,10},{10,1... | collective-permute-start | bytes 9437192 | tf_op jit(solution)/shard_map/ppermute | solution.py:69
  284.5 135.1 %collective-permute-start.2 = (bf16[1536,1024]{1,0:T(8,128)(2,1)}, bf16[1536,1024]{1,0:T(8,128)(2,1)S(1)}, u32[]{:S(2)}, u32[]{:S(2)}) collective-permute-start(bf16[1536,1024]{1,0:T(8,128)(2,1)} %collective-permute-done), channel_id=1, source_target_pairs={{0,1},{1,2},{2,3},{3,0},{4,5},{5,6},{6,7},{7,4},{8,9},{9,10},{10,1... | collective-permute-start | bytes 9437192 | tf_op jit(solution)/shard_map/ppermute | solution.py:69
  423.3 5.7 copy-start
  566.0 237.2 %reduce-scatter.5.cloned.1.call-start = ((), (), s32[]{:S(2)}) async-start(), calls=%async_computation.7 | async-start | bytes 18874368 | tf_op jit(solution)/shard_map/reduce_scatter | solution.py:95
  684.4 0.7 copy-start.4
  701.5 118.0 %all-to-all-start = ((f32[4,128,1024]{2,1,0:T(8,128)}), f32[4,128,1024]{2,1,0:T(8,128)S(1)}, u32[]{:S(2)}, u32[]{:S(2)}) async-start(f32[4,128,1024]{2,1,0:T(8,128)} %bitcast.111), calls=%async_computation.1 | async-start | bytes 4194304 | tf_op jit(solution)/shard_map/all_to_all | solution.py:105
  819.5 50.0 %all-to-all-start.2 = ((f32[4,128,1024]{2,1,0:T(8,128)}), f32[4,128,1024]{2,1,0:T(8,128)}, u32[]{:S(2)}, u32[]{:S(2)}) async-start(f32[4,128,1024]{2,1,0:T(8,128)} %bitcast.110), calls=%async_computation.4 | async-start | bytes 4194304 | tf_op jit(solution)/shard_map/all_to_all | solution.py:105
  869.4 51.6 %all-to-all-start.1 = ((f32[4,128,1024]{2,1,0:T(8,128)}), f32[4,128,1024]{2,1,0:T(8,128)S(1)}, u32[]{:S(2)}, u32[]{:S(2)}) async-start(f32[4,128,1024]{2,1,0:T(8,128)} %copy.31), calls=%async_computation.2 | async-start | bytes 4194304 | tf_op jit(solution)/shard_map/all_to_all | solution.py:107
  883.1 45.6 %copy-start.6 = (s32[2]{0:T(128)S(1)}, s32[2]{0:T(128)}, u32[]{:S(2)}) copy-start(s32[2]{0:T(128)} %param.13) | copy-start | bytes 28
  921.0 11.4 %copy-start.2 = (f32[4,128,1024]{2,1,0:T(8,128)}, f32[4,128,1024]{2,1,0:T(8,128)S(1)}, u32[]{:S(2)}) copy-start(f32[4,128,1024]{2,1,0:T(8,128)S(1)} %all-to-all-done.1) | copy-start | bytes 6291460
  921.0 52.2 %all-to-all-start.3 = ((f32[4,128,1024]{2,1,0:T(8,128)}), f32[4,128,1024]{2,1,0:T(8,128)}, u32[]{:S(2)}, u32[]{:S(2)}) async-start(f32[4,128,1024]{2,1,0:T(8,128)} %copy.36), calls=%async_computation.5 | async-start | bytes 4194304 | tf_op jit(solution)/shard_map/all_to_all | solution.py:107
Sparse Core Ops, SparseCore 0:
  566.1 117.2 reduce-scatter.2
  687.0 116.1 reduce-scatter.4
